TPU v7x, 32 devices: a whole 2x2x4 slice. The times are simulated.
32 devices in a mesh: shard: 4 (over y, x), ctx: 2 (over core), tp: 4 (over z).
Axes of the slice: x: 2, y: 2, z: 4, core: 2. Of those that a mesh axis runs over, the one named last changes fastest.
Arguments:
- activations: bfloat16 [4, 2048, 1024], P('shard', 'ctx'), may hold values from -6 to 6
- timestep: int32 [4], P('shard'), may hold values from 0 to 999
- positions: int32 [4, 2048], P('shard', 'ctx'), may hold values from 0 to 16383
- qkv_weight: bfloat16 [3, 1024, 1024], P(None, 'shard', 'tp'), may hold values from -0.1875 to 0.1875
- out_weight: bfloat16 [1024, 1024], P('tp', 'shard'), may hold values from -4 to 4
- up_weight: bfloat16 [1024, 4096], P('shard', 'tp'), may hold values from -0.1875 to 0.1875
- down_weight: bfloat16 [4096, 1024], P('tp', 'shard'), may hold values from -0.125 to 0.125
- time_weight: bfloat16 [256, 4, 1024], P(None, None, 'shard'), may hold values from -0.1875 to 0.1875
- norm_gains: bfloat16 [2, 1024], P(None, 'shard'), may hold values from 0.5 to 1.5
- cotangent: bfloat16 [4, 2048, 1024], P('shard', 'ctx'), may hold values from -6 to 6
Outputs:
- output: bfloat16 [4, 2048, 1024], P('shard', 'ctx')
- input_grad: bfloat16 [4, 2048, 1024], P('shard', 'ctx')
- grad_qkv: float32 [3, 1024, 1024], P(None, 'shard', 'tp')
- grad_out: float32 [1024, 1024], P('tp', 'shard')
- grad_up: float32 [1024, 4096], P('shard', 'tp')
- grad_down: float32 [4096, 1024], P('tp', 'shard')
- grad_time: float32 [256, 4, 1024], P(None, None, 'shard')
- grad_gains: float32 [2, 1024], P(None, 'shard')
All inputs are finite; a program needn't handle non-finite values.
Results may differ from a plain program's by a relative error of at most 0.015.
Values may be sent and summed in bfloat16 or wider, within the bound.
No kernel may reach another device: no remote copies, remote signals or barrier semaphores. Data moves between devices by JAX's collectives and lax.ppermute only.
A program may use at most 320 MiB of HBM per device.

v0:
```python
from functools import partial
import math
import jax
import jax.numpy as jnp
from jax import lax
from jax.sharding import PartitionSpec as P

HEAD_DIM = 64
TEMB = 256
highest = lax.Precision.HIGHEST
norm_epsilon = 1e-05


def embed_time(timestep):
    half_width = TEMB // 2
    frequency = jnp.exp(-math.log(10000.0) * jnp.arange(half_width, dtype=jnp.float32) / half_width)
    angles = timestep.astype(jnp.float32)[:, None] * frequency[None, :]
    return jnp.concatenate([jnp.sin(angles), jnp.cos(angles)], axis=-1)


def rotary_tables(positions):
    half_width = HEAD_DIM // 2
    frequency = jnp.exp(-math.log(10000.0) * jnp.arange(half_width, dtype=jnp.float32) / half_width)
    angles = positions.astype(jnp.float32)[..., None] * frequency
    return (jnp.cos(angles), jnp.sin(angles))


def rotate(heads_in, cosines, sines):
    half_width = HEAD_DIM // 2
    first = heads_in[..., :half_width]
    second = heads_in[..., half_width:]
    cos_wide = cosines[..., None, :]
    sin_wide = sines[..., None, :]
    return jnp.concatenate(
        [first * cos_wide - second * sin_wide, second * cos_wide + first * sin_wide], axis=-1
    )


def unrotate(heads_in, cosines, sines):
    half_width = HEAD_DIM // 2
    first = heads_in[..., :half_width]
    second = heads_in[..., half_width:]
    cos_wide = cosines[..., None, :]
    sin_wide = sines[..., None, :]
    return jnp.concatenate(
        [first * cos_wide + second * sin_wide, second * cos_wide - first * sin_wide], axis=-1
    )


def scaled_norm(values, gain_vec, scaling, offset):
    centered = values - jnp.mean(values, axis=-1, keepdims=True)
    variance = jnp.mean(centered * centered, axis=-1, keepdims=True)
    inverse_std = lax.rsqrt(variance + norm_epsilon)
    normed = centered * inverse_std
    return (
        normed * gain_vec * (1.0 + scaling[:, None, :]) + offset[:, None, :],
        normed,
        inverse_std,
    )


def norm_back(grad_in, normed, inverse_std, gain_vec, scaling):
    factor = gain_vec * (1.0 + scaling[:, None, :])
    grad_normed = grad_in * factor
    grad_values = inverse_std * (
        grad_normed
        - jnp.mean(grad_normed, axis=-1, keepdims=True)
        - normed * jnp.mean(grad_normed * normed, axis=-1, keepdims=True)
    )
    grad_gain = jnp.sum(grad_in * normed * (1.0 + scaling[:, None, :]), axis=(0, 1))
    grad_scaling = jnp.sum(grad_in * normed * gain_vec, axis=1)
    grad_offset = jnp.sum(grad_in, axis=1)
    return (grad_values, grad_gain, grad_scaling, grad_offset)


def group_heads(field, per_group):
    seq_count, rows_count, _ = field.shape
    split = field.reshape(seq_count, rows_count, -1, HEAD_DIM).transpose(0, 2, 1, 3)
    return split.reshape(-1, per_group, rows_count, HEAD_DIM)


def ungroup_heads(field, seq_count):
    rows_count = field.shape[2]
    joined = field.reshape(seq_count, -1, rows_count, HEAD_DIM).transpose(0, 2, 1, 3)
    return joined.reshape(seq_count, rows_count, -1)


def attend_block(triple, scaling):
    queries, keys, values = triple
    scores = jnp.einsum("gqd,gkd->gqk", queries, keys, preferred_element_type=jnp.float32) * scaling
    top_score = jnp.max(scores, axis=-1, keepdims=True)
    raised = jnp.exp(scores - top_score)
    total = jnp.sum(raised, axis=-1, keepdims=True)
    weights = (raised / total).astype(jnp.bfloat16)
    attended = jnp.einsum("gqk,gkd->gqd", weights, values, preferred_element_type=jnp.float32)
    return (attended, (top_score + jnp.log(total))[..., 0])


def attend_back(bundle, scaling):
    queries, keys, values, grad_out, log_total = bundle
    scores = jnp.einsum("gqd,gkd->gqk", queries, keys, preferred_element_type=jnp.float32) * scaling
    weights = jnp.exp(scores - log_total[..., None])
    grad_values = jnp.einsum(
        "gqk,gqd->gkd", weights.astype(jnp.bfloat16), grad_out, preferred_element_type=jnp.float32
    )
    grad_weights = jnp.einsum("gqd,gkd->gqk", grad_out, values, preferred_element_type=jnp.float32)
    row_term = jnp.sum(weights * grad_weights, axis=-1, keepdims=True)
    grad_scores = (weights * (grad_weights - row_term)).astype(jnp.bfloat16)
    grad_queries = (
        jnp.einsum("gqk,gkd->gqd", grad_scores, keys, preferred_element_type=jnp.float32) * scaling
    )
    grad_keys = (
        jnp.einsum("gqk,gqd->gkd", grad_scores, queries, preferred_element_type=jnp.float32)
        * scaling
    )
    return (grad_queries, grad_keys, grad_values)


def gelu_slope(hidden):
    return (
        0.5 * (1.0 + lax.erf(hidden * 0.7071067811865476))
        + hidden * jnp.exp(-0.5 * hidden * hidden) * 0.3989422804014327
    )


def body(
    activations,
    timestep,
    positions,
    qkv_weight,
    out_weight,
    up_weight,
    down_weight,
    time_weight,
    norm_gains,
    cotangent,
):
    seq_count, tokens, width = activations.shape
    local_width = qkv_weight.shape[2]
    heads_local = local_width // HEAD_DIM
    per_group = min(heads_local, max(1, 512 // tokens))
    while heads_local % per_group:
        per_group -= 1
    scaling = HEAD_DIM ** (-0.5)
    full_qkv, full_out, full_up, full_down, full_time, full_gains = (
        lax.all_gather(qkv_weight, "shard", axis=1, tiled=True),
        lax.all_gather(out_weight, "shard", axis=1, tiled=True),
        lax.all_gather(up_weight, "shard", axis=0, tiled=True),
        lax.all_gather(down_weight, "shard", axis=1, tiled=True),
        lax.all_gather(time_weight, "shard", axis=2, tiled=True),
        lax.all_gather(norm_gains, "shard", axis=1, tiled=True),
    )
    gains_f = full_gains.astype(jnp.float32)
    embedding = embed_time(timestep)
    modulation = jnp.einsum(
        "sk,kcd->scd", embedding, full_time.astype(jnp.float32), precision=highest
    )
    cosines, sines = rotary_tables(positions)
    inputs_f = activations.astype(jnp.float32)
    first_out, normed_one, inverse_one = scaled_norm(
        inputs_f, gains_f[0], modulation[:, 0], modulation[:, 1]
    )
    first_low = first_out.astype(jnp.bfloat16)
    projected = jnp.einsum("std,cde->cste", first_low, full_qkv, preferred_element_type=jnp.float32)
    head_shape = (seq_count, tokens, heads_local, HEAD_DIM)
    query_rot = (
        rotate(projected[0].reshape(head_shape), cosines, sines)
        .reshape(seq_count, tokens, local_width)
        .astype(jnp.bfloat16)
    )
    key_rot = (
        rotate(projected[1].reshape(head_shape), cosines, sines)
        .reshape(seq_count, tokens, local_width)
        .astype(jnp.bfloat16)
    )
    value_low = projected[2].astype(jnp.bfloat16)
    keys_all, values_all = (
        lax.all_gather(key_rot, "ctx", axis=1, tiled=True),
        lax.all_gather(value_low, "ctx", axis=1, tiled=True),
    )
    query_groups = group_heads(query_rot, per_group)
    attended, log_total = lax.map(
        partial(attend_block, scaling=scaling),
        (query_groups, group_heads(keys_all, per_group), group_heads(values_all, per_group)),
    )
    attended_low = ungroup_heads(attended, seq_count).astype(jnp.bfloat16)
    branch_part = jnp.einsum(
        "ste,ed->std", attended_low, full_out, preferred_element_type=jnp.float32
    )
    middle = inputs_f + lax.psum(branch_part, "tp")
    second_out, normed_two, inverse_two = scaled_norm(
        middle, gains_f[1], modulation[:, 2], modulation[:, 3]
    )
    second_low = second_out.astype(jnp.bfloat16)
    hidden = jnp.einsum("std,df->stf", second_low, full_up, preferred_element_type=jnp.float32)
    activated = jax.nn.gelu(hidden, approximate=False).astype(jnp.bfloat16)
    mlp_part = jnp.einsum("stf,fd->std", activated, full_down, preferred_element_type=jnp.float32)
    output = (middle + lax.psum(mlp_part, "tp")).astype(jnp.bfloat16)
    back_qkv, back_out, back_up, back_down = (
        lax.all_gather(qkv_weight, "shard", axis=1, tiled=True),
        lax.all_gather(out_weight, "shard", axis=1, tiled=True),
        lax.all_gather(up_weight, "shard", axis=0, tiled=True),
        lax.all_gather(down_weight, "shard", axis=1, tiled=True),
    )
    keys_back, values_back = (
        lax.all_gather(key_rot, "ctx", axis=1, tiled=True),
        lax.all_gather(value_low, "ctx", axis=1, tiled=True),
    )
    grad_down = jnp.einsum("stf,std->fd", activated, cotangent, preferred_element_type=jnp.float32)
    grad_act = jnp.einsum("std,fd->stf", cotangent, back_down, preferred_element_type=jnp.float32)
    grad_hidden = (grad_act * gelu_slope(hidden)).astype(jnp.bfloat16)
    grad_up = jnp.einsum("std,stf->df", second_low, grad_hidden, preferred_element_type=jnp.float32)
    grad_second = lax.psum(
        jnp.einsum("stf,df->std", grad_hidden, back_up, preferred_element_type=jnp.float32), "tp"
    )
    grad_mid_norm, gain_two, scaling_two, offset_two = norm_back(
        grad_second, normed_two, inverse_two, gains_f[1], modulation[:, 2]
    )
    grad_middle = cotangent.astype(jnp.float32) + grad_mid_norm
    grad_branch = grad_middle.astype(jnp.bfloat16)
    grad_out = jnp.einsum(
        "ste,std->ed", attended_low, grad_branch, preferred_element_type=jnp.float32
    )
    grad_attended = jnp.einsum(
        "std,ed->ste", grad_branch, back_out, preferred_element_type=jnp.float32
    ).astype(jnp.bfloat16)
    grad_query_g, grad_key_g, grad_value_g = lax.map(
        partial(attend_back, scaling=scaling),
        (
            query_groups,
            group_heads(keys_back, per_group),
            group_heads(values_back, per_group),
            group_heads(grad_attended, per_group),
            log_total,
        ),
    )
    grad_key_all = ungroup_heads(grad_key_g, seq_count)
    grad_value_all = ungroup_heads(grad_value_g, seq_count)
    grad_key, grad_value = (
        lax.psum_scatter(grad_key_all, "ctx", scatter_dimension=1, tiled=True),
        lax.psum_scatter(grad_value_all, "ctx", scatter_dimension=1, tiled=True),
    )
    grad_query = ungroup_heads(grad_query_g, seq_count)
    query_back = unrotate(grad_query.reshape(head_shape), cosines, sines).reshape(
        seq_count, tokens, local_width
    )
    key_back = unrotate(grad_key.reshape(head_shape), cosines, sines).reshape(
        seq_count, tokens, local_width
    )
    grad_projected = jnp.stack([query_back, key_back, grad_value], axis=0).astype(jnp.bfloat16)
    grad_qkv = jnp.einsum(
        "std,cste->cde", first_low, grad_projected, preferred_element_type=jnp.float32
    )
    grad_first = lax.psum(
        jnp.einsum("cste,cde->std", grad_projected, back_qkv, preferred_element_type=jnp.float32),
        "tp",
    )
    grad_in_norm, gain_one, scaling_one, offset_one = norm_back(
        grad_first, normed_one, inverse_one, gains_f[0], modulation[:, 0]
    )
    input_grad = (grad_middle + grad_in_norm).astype(jnp.bfloat16)
    grad_modulation = jnp.stack([scaling_one, offset_one, scaling_two, offset_two], axis=1)
    grad_time = jnp.einsum("sk,scd->kcd", embedding, grad_modulation, precision=highest)
    grad_gains = jnp.stack([gain_one, gain_two], axis=0)
    shares = (
        lax.psum_scatter(grad_qkv, "shard", scatter_dimension=1, tiled=True),
        lax.psum_scatter(grad_out, "shard", scatter_dimension=1, tiled=True),
        lax.psum_scatter(grad_up, "shard", scatter_dimension=0, tiled=True),
        lax.psum_scatter(grad_down, "shard", scatter_dimension=1, tiled=True),
        lax.psum_scatter(grad_time, "shard", scatter_dimension=2, tiled=True),
        lax.psum_scatter(grad_gains, "shard", scatter_dimension=1, tiled=True),
    )
    shares = lax.psum((shares[0], shares[1], shares[2], shares[3], shares[4], shares[5]), "ctx")
    return (output, input_grad, shares[0], shares[1], shares[2], shares[3], shares[4], shares[5])


def solution(mesh):
    placed = (
        P("shard", "ctx", None),
        P("shard"),
        P("shard", "ctx"),
        P(None, "shard", "tp"),
        P("tp", "shard"),
        P("shard", "tp"),
        P("tp", "shard"),
        P(None, None, "shard"),
        P(None, "shard"),
        P("shard", "ctx", None),
    )
    return jax.shard_map(
        body,
        mesh=mesh,
        in_specs=placed,
        out_specs=(
            P("shard", "ctx", None),
            P("shard", "ctx", None),
            P(None, "shard", "tp"),
            P("tp", "shard"),
            P("shard", "tp"),
            P("tp", "shard"),
            P(None, None, "shard"),
            P(None, "shard"),
        ),
        check_vma=False,
    )
```

profile of v0, /device:TPU:0, one launch (start us, length us, event | category | flops | bytes accessed | tf_op | source)
XLA Modules:
  0.0 1433.2 jit_solution(13286509616975945891)
XLA Ops:
  11.3 9.6 all_gather.30
  24.3 23.4 %all-gather.8.cloned.1.call-done = bf16[256,4,1024]{2,1,0:T(4,128)(2,1)} async-done(((bf16[256,4,256]{2,1,0:T(4,128)(2,1)}), bf16[256,4,1024]{2,1,0:T(4,128)(2,1)}) %all-gather.8.cloned.1.call-update) | async-done | bytes 2097168 | tf_op jit(solution)/shard_map/all_gather | solution.py:150
  47.7 3.4 fusion.90
  51.8 29.2 %all-gather.10.cloned.1.call-done = bf16[3,1024,256]{1,2,0:T(8,128)(2,1)} async-done(((bf16[3,256,256]{1,2,0:T(8,128)(2,1)}), bf16[3,1024,256]{1,2,0:T(8,128)(2,1)}) %all-gather.10.cloned.1.call-update) | async-done | bytes 1572880 | tf_op jit(solution)/shard_map/all_gather | solution.py:146
  81.0 3.4 convolution_bitcast_fusion.5
  88.6 14.1 all_gather.35
  105.9 2.9 copy.45
  108.8 2.7 copy.43
  111.5 35.0 %while.28 = (s32[]{:T(128)}, bf16[4,1,1024,64]{2,3,1,0:T(8,128)(2,1)}, f32[4,1,1024]{2,1,0:T(1,128)S(1)}, bf16[4,1,1024,64]{3,2,1,0:T(8,128)(2,1)S(1)}, bf16[4,1...) while((s32[]{:T(128)}, bf16[4,1,1024,64]{2,3,1,0:T(8,128)(2,1)}, ...), condition=%wide.region_5.6_spmd.clone, body=%wide.region_2.5_spmd.sunk.clone | while | flops 555744256 | bytes 30976136 | solution.py:182
  111.5 2.4 multiply_reduce_fusion.14
  115.8 3.6 fusion.162
  120.2 2.4 multiply_reduce_fusion.14
  124.6 3.6 fusion.162
  129.0 2.4 multiply_reduce_fusion.14
  133.3 3.6 fusion.162
  137.7 2.4 multiply_reduce_fusion.14
  142.1 3.6 fusion.162
  146.5 4.0 convolution_bitcast_fusion.3
  151.9 153.9 %all-reduce.7.cloned.1.call-done = f32[1,1024,1024]{2,1,0:T(8,128)} async-done(((f32[1,1024,1024]{2,1,0:T(8,128)}), f32[1,1024,1024]{2,1,0:T(8,128)}) %all-reduce.7.cloned.1.call-update) | async-done | bytes 4194320 | tf_op jit(solution)/shard_map/psum | solution.py:190
  305.7 2.7 fusion.110
  311.0 31.0 %all-gather.14.cloned.1.call-done = bf16[1024,1024]{1,0:T(8,128)(2,1)} async-done(((bf16[256,1024]{1,0:T(8,128)(2,1)}), bf16[1024,1024]{1,0:T(8,128)(2,1)}) %all-gather.14.cloned.1.call-update) | async-done | bytes 2097168 | tf_op jit(solution)/shard_map/all_gather | solution.py:148
  342.0 15.0 %fusion.66 = (bf16[1024,1024]{1,0:T(8,128)(2,1)}, f32[1024,1024]{1,0:T(8,128)}) fusion(bf16[1024,1024]{1,0:T(8,128)(2,1)} %all-gather.14.cloned.1.call-done, f32[1,1024,1024]{2,1,0:T(8,128)} %copy-done, f32[1024]{0:T(1024)S(1)} %bitcast.301, f32[1024]{0:T(1024)S(1)} %bitcast.283, f32[1024]{0:T(1024)S(1)} %bitcast.279, f32[1024]{0:T(1024)S(1)} %add_rsqrt_fusion, ...), kind=kOutput, calls=%fused_computation.77 | convolution fusion | flops 2221932544 | bytes 12603392 | tf_op jit(solution)/shard_map/std,df->stf/dot_general | solution.py:195
  356.9 22.2 %all-gather.16.cloned.1.call-done = bf16[1024,1024]{1,0:T(8,128)(2,1)} async-done(((bf16[1024,256]{1,0:T(8,128)(2,1)}), bf16[1024,1024]{1,0:T(8,128)(2,1)}) %all-gather.16.cloned.1.call-update) | async-done | bytes 2097168 | tf_op jit(solution)/shard_map/all_gather | solution.py:149
  379.1 6.0 fusion.72
  386.5 4.4 convolution_bitcast_fusion.1
  391.3 154.9 %all-reduce.9.cloned.1.call-done = f32[1,1024,1024]{2,1,0:T(8,128)} async-done(((f32[1,1024,1024]{2,1,0:T(8,128)}), f32[1,1024,1024]{2,1,0:T(8,128)}) %all-reduce.9.cloned.1.call-update) | async-done | bytes 4194320 | tf_op jit(solution)/shard_map/psum | solution.py:213
  546.1 6.2 multiply_reduce_fusion.2
  557.6 2.4 copy.46
  560.0 51.6 %while.29 = (s32[]{:T(128)}, f32[4,1,1024,64]{2,3,1,0:T(8,128)}, f32[4,1,2048,64]{2,3,1,0:T(8,128)}, f32[4,1,2048,64]{2,3,1,0:T(8,128)}, bf16[4,1,1024,64]{3,2,1...) while((s32[]{:T(128)}, f32[4,1,1024,64]{2,3,1,0:T(8,128)}, ...), condition=%wide.region_15.16_spmd.clone, body=%wide.region_13.15_spmd.sunk.clone | while | flops 1367538688 | bytes 68977792 | solution.py:227
  561.3 2.5 fusion.174
  563.7 3.2 multiply_reduce_fusion.15
  574.2 2.4 fusion.174
  576.6 3.2 multiply_reduce_fusion.15
  587.1 2.4 fusion.174
  589.5 3.2 multiply_reduce_fusion.15
  599.9 2.4 fusion.174
  602.4 3.2 multiply_reduce_fusion.15
  605.5 2.2 multiply_convert_fusion.3
  611.7 2.9 copy.49
  615.1 7.3 convolution_bitcast_fusion.2
  624.5 9.5 reduce-scatter.15.cloned.1.call-done
  635.3 5.2 convolution_bitcast_fusion
  641.2 292.3 %all-reduce.11.cloned.1.call-done = (f32[1,1024,1024]{2,1,0:T(8,128)}, f32[1,1024,1024]{2,1,0:T(8,128)}) async-done(((f32[1,1024,1024]{2,1,0:T(8,128)}, f32[1,1024,1024]{2,1,0:T(8,128)}), (f32[1,1024,1024]{2,1,0:T(8,128)}, f32[1,1024,1024]{2,1,0:T(8,128)})) %all-reduce.11.cloned.1.call-update) | async-done | bytes 8388624 | tf_op jit(solution)/shard_map/psum | solution.py:198
  933.5 4.2 multiply_reduce_fusion.3
  937.7 2.6 broadcast_multiply_fusion
  940.3 64.8 %copy.59 = f32[256,4,1024]{1,0,2:T(8,128)} copy(f32[256,4,1024]{2,1,0:T(4,128)} %broadcast_multiply_fusion) | data formatting | bytes 8388608
  1005.1 110.5 %reshape.619 = f32[1024,1024]{1,0:T(8,128)} reshape(f32[1024,256,4]{2,1,0:T(8,128)} %bitcast.86) | data formatting | bytes 8388608
  1116.6 3.9 fusion.83
  1120.6 7.2 fusion.87
  1128.5 7.7 fusion.106
  1137.3 4.8 convolution_bitcast_fusion.4
  1143.3 24.2 %reduce-scatter.25.cloned.1.call-done = f32[256,1024]{1,0:T(8,128)} async-done(((f32[1024,1024]{1,0:T(8,128)}), f32[256,1024]{1,0:T(8,128)}) %reduce-scatter.25.cloned.1.call-update) | async-done | bytes 1048592
  1167.5 36.8 %reshape.620 = f32[256,256,4]{2,1,0:T(8,128)} reshape(f32[256,1024]{1,0:T(8,128)} %reduce-scatter.25.cloned.1.call-done) | data formatting | bytes 2097152
  1204.3 21.0 %copy.60 = f32[256,4,256]{2,1,0:T(4,128)} copy(f32[256,4,256]{1,0,2:T(8,128)} %bitcast.252) | data formatting | bytes 2097152
  1225.3 29.1 %reduce-scatter.23.cloned.1.call-done = f32[1024,256]{1,0:T(8,128)} async-done(((f32[1024,1024]{1,0:T(8,128)}), f32[1024,256]{1,0:T(8,128)}) %reduce-scatter.23.cloned.1.call-update) | async-done | bytes 1048592 | tf_op jit(solution)/shard_map/reduce_scatter | solution.py:269
  1254.5 55.8 %reduce-scatter.21.cloned.1.call-done = f32[256,1024]{1,0:T(8,128)} async-done(((f32[1024,1024]{1,0:T(8,128)}), f32[256,1024]{1,0:T(8,128)}) %reduce-scatter.21.cloned.1.call-update) | async-done | bytes 1048592 | tf_op jit(solution)/shard_map/reduce_scatter | solution.py:268
  1310.3 46.8 %reduce-scatter.17.cloned.1.call-done = f32[3,256,256]{1,2,0:T(8,128)} async-done(((f32[3,1024,256]{1,2,0:T(8,128)}), f32[3,256,256]{1,2,0:T(8,128)}) %reduce-scatter.17.cloned.1.call-update) | async-done | bytes 786448 | tf_op jit(solution)/shard_map/reduce_scatter | solution.py:266
  1357.2 5.7 add_convert_fusion
  1363.8 2.5 fusion.62
  1366.4 18.8 %reduce-scatter.27.cloned.1.call-done = f32[256,2]{1,0:T(8,128)} async-done(((f32[1024,2]{1,0:T(8,128)}), f32[256,2]{1,0:T(8,128)}) %reduce-scatter.27.cloned.1.call-update) | async-done | bytes 2064
  1386.1 3.0 psum.79
  1389.2 28.7 %all-reduce.13.cloned.1.call-done = (f32[3,256,256]{1,2,0:T(8,128)}, f32[256,256]{1,0:T(8,128)}, f32[256,1024]{1,0:T(8,128)}, f32[1024,256]{1,0:T(8,128)}, f32[256,4,256]{2,1,0:T(4,128)}) async-done(((f32[3,256,256]{1,2,0:T(8,128)}, f32[256,256]{1,0:T(8,128)}, f32[256,1024]{1,0:T(8,128)}, f32[1024,256]{1,0:T(8,128)}, f32[256,4,256]{2,1,0:T(4,128)}), (f32[3,256,256]{1,2,0:T(8,128)}, f32[256,256]{1,0:T(8,128)}, ...) | async-done | bytes 4194320 | tf_op jit(solution)/shard_map/psum | solution.py:273
  1417.8 2.4 copy.54
  1421.9 2.3 copy.108
  (246 shorter events, 77.3 us)
Async XLA Ops:
  7.2 15.8 %copy-start.4 = (bf16[1,1024,1024]{2,1,0:T(8,128)(2,1)S(1)}, bf16[1,1024,1024]{2,1,0:T(8,128)(2,1)}, u32[]{:S(2)}) copy-start(bf16[1,1024,1024]{2,1,0:T(8,128)(2,1)} %param.14) | copy-start | bytes 6291460
  7.2 40.6 %all-gather.8.cloned.1.call-start = ((), (), s32[]{:S(2)}) async-start(), calls=%async_computation.8 | async-start | bytes 2621440 | tf_op jit(solution)/shard_map/all_gather | solution.py:150
  7.9 73.1 %all-gather.10.cloned.1.call-start = ((), (), s32[]{:S(2)}) async-start(), calls=%async_computation.9 | async-start | bytes 1966080 | tf_op jit(solution)/shard_map/all_gather | solution.py:146
  9.9 96.0 %all-gather.12.cloned.1.call-start = ((), (), s32[]{:S(2)}) async-start(), calls=%async_computation.10 | async-start | bytes 1572864 | tf_op jit(solution)/shard_map/all_gather | solution.py:178
  21.0 26.8 %copy-start.51 = (f32[1,128]{1,0:T(1,128)}, f32[1,128]{1,0:T(1,128)S(1)}, u32[]{:S(2)}) copy-start(f32[1,128]{1,0:T(1,128)S(1)} %get-tuple-element.244) | copy-start | bytes 1540
  21.0 30.2 %copy-start.49 = (f32[1,128]{1,0:T(1,128)}, f32[1,128]{1,0:T(1,128)S(1)}, u32[]{:S(2)}) copy-start(f32[1,128]{1,0:T(1,128)S(1)} %get-tuple-element.243) | copy-start | bytes 1540
  23.0 61.4 %copy-start.29 = (f32[1024]{0:T(1024)}, f32[1024]{0:T(1024)S(1)}, u32[]{:S(2)}) copy-start(f32[1024]{0:T(1024)S(1)} %broadcast_multiply_fusion.6) | copy-start | bytes 12292
  23.7 60.7 %copy-start.33 = (f32[1024]{0:T(1024)}, f32[1024]{0:T(1024)S(1)}, u32[]{:S(2)}) copy-start(f32[1024]{0:T(1024)S(1)} %add_rsqrt_fusion.1) | copy-start | bytes 12292
  23.8 60.7 %copy-start.41 = (f32[1,1024]{1,0:T(1,128)}, f32[1,1024]{1,0:T(1,128)S(1)}, u32[]{:S(2)}) copy-start(f32[1,1024]{1,0:T(1,128)S(1)} %get-tuple-element.240) | copy-start | bytes 12292
  23.8 522.3 %copy-start.36 = (f32[1,1024]{1,0:T(1,128)}, f32[1,1024]{1,0:T(1,128)S(1)}, u32[]{:S(2)}) copy-start(f32[1,1024]{1,0:T(1,128)S(1)} %get-tuple-element.239) | copy-start | bytes 12292
  24.3 60.4 %copy-start.16 = (f32[1024,32]{0,1:T(8,128)}, f32[1024,32]{0,1:T(8,128)S(1)}, u32[]{:S(2)}) copy-start(f32[1024,32]{0,1:T(8,128)S(1)} %get-tuple-element.237) | copy-start | bytes 393220
  24.3 60.4 %copy-start.18 = (f32[1024,32]{0,1:T(8,128)}, f32[1024,32]{0,1:T(8,128)S(1)}, u32[]{:S(2)}) copy-start(f32[1024,32]{0,1:T(8,128)S(1)} %get-tuple-element.238) | copy-start | bytes 393220
  51.2 33.3 %copy-start.45 = (f32[1,1,1024]{2,0,1:T(1,128)}, f32[1,1,1024]{2,0,1:T(1,128)S(1)}, u32[]{:S(2)}) copy-start(f32[1,1,1024]{2,0,1:T(1,128)S(1)} %get-tuple-element.236) | copy-start | bytes 12292
  51.2 290.7 %copy-start.47 = (f32[1,1,1024]{2,0,1:T(1,128)}, f32[1,1,1024]{2,0,1:T(1,128)S(1)}, u32[]{:S(2)}) copy-start(f32[1,1,1024]{2,0,1:T(1,128)S(1)} %get-tuple-element.235) | copy-start | bytes 12292
  51.8 32.6 %copy-start.43 = (f32[1,1,1024]{2,1,0:T(1,128)}, f32[1,1,1024]{2,1,0:T(1,128)S(1)}, u32[]{:S(2)}) copy-start(f32[1,1,1024]{2,1,0:T(1,128)S(1)} %get-tuple-element.234) | copy-start | bytes 12292
  51.8 494.3 %copy-start.39 = (f32[1,1,1024]{2,1,0:T(1,128)}, f32[1,1,1024]{2,1,0:T(1,128)S(1)}, u32[]{:S(2)}) copy-start(f32[1,1,1024]{2,1,0:T(1,128)S(1)} %get-tuple-element.233) | copy-start | bytes 12292
  84.5 1.8 copy-start.14
  84.7 3.8 copy-start.26
  86.3 22.4 %all-gather.18.cloned.1.call-start = ((), (), s32[]{:S(2)}) async-start(), calls=%async_computation.21 | async-start | bytes 1572864 | tf_op jit(solution)/shard_map/all_gather | solution.py:179
  88.5 217.2 %all-reduce.7.cloned.1.call-start = ((), (), s32[]{:S(2)}) async-start(), calls=%async_computation.11 | async-start | bytes 8388608 | tf_op jit(solution)/shard_map/psum | solution.py:190
  113.9 2.0 copy-start.10
  122.6 2.0 copy-start.10
  131.4 2.0 copy-start.10
  140.1 2.0 copy-start.10
  150.5 191.5 %all-gather.14.cloned.1.call-start = ((), (), s32[]{:S(2)}) async-start(), calls=%async_computation.12 | async-start | bytes 2621440 | tf_op jit(solution)/shard_map/all_gather | solution.py:148
  151.1 228.0 %all-gather.16.cloned.1.call-start = ((), (), s32[]{:S(2)}) async-start(), calls=%async_computation.13 | async-start | bytes 2621440 | tf_op jit(solution)/shard_map/all_gather | solution.py:149
  151.8 394.3 %all-reduce.9.cloned.1.call-start = ((), (), s32[]{:S(2)}) async-start(), calls=%async_computation.14 | async-start | bytes 8388608 | tf_op jit(solution)/shard_map/psum | solution.py:213
  308.4 2.0 copy-start
  308.4 243.9 %copy-start.27 = (f32[1024]{0:T(1024)}, f32[1024]{0:T(1024)S(1)}, u32[]{:S(2)}) copy-start(f32[1024]{0:T(1024)S(1)} %broadcast_multiply_fusion.5) | copy-start | bytes 12292
  311.0 241.4 %copy-start.31 = (f32[1024]{0:T(1024)}, f32[1024]{0:T(1024)S(1)}, u32[]{:S(2)}) copy-start(f32[1024]{0:T(1024)S(1)} %add_rsqrt_fusion) | copy-start | bytes 12292
  342.0 37.2 %copy-start.15 = (bf16[1,1024,1024]{2,1,0:T(8,128)(2,1)S(1)}, bf16[1,1024,1024]{2,1,0:T(8,128)(2,1)}, u32[]{:S(2)}) copy-start(bf16[1,1024,1024]{2,1,0:T(8,128)(2,1)} %param.23) | copy-start | bytes 6291460
  379.1 7.4 copy-start.53
  385.1 1.4 copy-start.54
  391.0 231.4 %reduce-scatter.13.cloned.1.call-start = ((), (), s32[]{:S(2)}) async-start(), calls=%async_computation.15 | async-start | bytes 3145728 | tf_op jit(solution)/shard_map/reduce_scatter | solution.py:240
  546.1 6.3 copy-start.1
  546.1 6.3 copy-start.7
  552.4 3.7 copy-start.13
  554.1 2.0 copy-start.2
  556.1 3.9 copy-start.6
  611.6 22.4 %reduce-scatter.15.cloned.1.call-start = ((), (), s32[]{:S(2)}) async-start(), calls=%async_computation.16 | async-start | bytes 3145728 | tf_op jit(solution)/shard_map/reduce_scatter | solution.py:241
  614.6 318.9 %all-reduce.11.cloned.1.call-start = ((), (), s32[]{:S(2)}) async-start(), calls=%async_computation.24 | async-start | bytes 16777216 | tf_op jit(solution)/shard_map/psum | solution.py:198
  615.0 7.4 copy-start.17
  615.0 7.3 copy-start.19
  615.1 7.3 copy-start.22
  624.2 16.3 %copy-start.23 = (bf16[1,1024,256]{2,1,0:T(8,128)(2,1)}, bf16[1,1024,256]{2,1,0:T(8,128)(2,1)S(1)}, u32[]{:S(2)}) copy-start(bf16[1,1024,256]{2,1,0:T(8,128)(2,1)S(1)} %copy.50) | copy-start | bytes 1572868
  624.4 16.1 %copy-start.25 = (bf16[1,1024,256]{2,1,0:T(8,128)(2,1)}, bf16[1,1024,256]{2,1,0:T(8,128)(2,1)S(1)}, u32[]{:S(2)}) copy-start(bf16[1,1024,256]{2,1,0:T(8,128)(2,1)S(1)} %copy.51) | copy-start | bytes 1572868
  640.5 292.9 %copy-start.5 = (bf16[1,1024,1024]{2,1,0:T(8,128)(2,1)S(1)}, bf16[1,1024,1024]{2,1,0:T(8,128)(2,1)}, u32[]{:S(2)}) copy-start(bf16[1,1024,1024]{2,1,0:T(8,128)(2,1)} %param.14) | copy-start | bytes 6291460
  640.5 292.9 %copy-start.30 = (f32[1024]{0:T(1024)S(1)}, f32[1024]{0:T(1024)}, u32[]{:S(2)}) copy-start(f32[1024]{0:T(1024)} %copy-done.29) | copy-start | bytes 12292
  640.5 292.9 %copy-start.34 = (f32[1024]{0:T(1024)S(1)}, f32[1024]{0:T(1024)}, u32[]{:S(2)}) copy-start(f32[1024]{0:T(1024)} %copy-done.33) | copy-start | bytes 12292
  640.5 292.9 %copy-start.35 = (f32[1,1,1024]{2,1,0:T(1,128)S(1)}, f32[1,1,1024]{2,1,0:T(1,128)}, u32[]{:S(2)}) copy-start(f32[1,1,1024]{2,1,0:T(1,128)} %get-tuple-element.231) | copy-start | bytes 12292
  640.6 292.9 %copy-start.42 = (f32[1,1024]{1,0:T(1,128)S(1)}, f32[1,1024]{1,0:T(1,128)}, u32[]{:S(2)}) copy-start(f32[1,1024]{1,0:T(1,128)} %copy-done.41) | copy-start | bytes 12292
  640.6 292.9 %copy-start.44 = (f32[1,1,1024]{2,1,0:T(1,128)S(1)}, f32[1,1,1024]{2,1,0:T(1,128)}, u32[]{:S(2)}) copy-start(f32[1,1,1024]{2,1,0:T(1,128)} %copy-done.43) | copy-start | bytes 12292
  640.6 526.9 %reduce-scatter.25.cloned.1.call-start = ((), (), s32[]{:S(2)}) async-start(), calls=%async_computation.22 | async-start | bytes 5242880
  1115.6 109.7 %reduce-scatter.19.cloned.1.call-start = ((), (), s32[]{:S(2)}) async-start(), calls=%async_computation.18 | async-start | bytes 1310720 | tf_op jit(solution)/shard_map/reduce_scatter | solution.py:267
  1120.5 134.0 %reduce-scatter.23.cloned.1.call-start = ((), (), s32[]{:S(2)}) async-start(), calls=%async_computation.20 | async-start | bytes 5242880 | tf_op jit(solution)/shard_map/reduce_scatter | solution.py:269
  1127.9 182.4 %reduce-scatter.21.cloned.1.call-start = ((), (), s32[]{:S(2)}) async-start(), calls=%async_computation.19 | async-start | bytes 5242880 | tf_op jit(solution)/shard_map/reduce_scatter | solution.py:268
  1136.3 5.9 copy-start.38
  1136.3 220.8 %reduce-scatter.17.cloned.1.call-start = ((), (), s32[]{:S(2)}) async-start(), calls=%async_computation.17 | async-start | bytes 3932160 | tf_op jit(solution)/shard_map/reduce_scatter | solution.py:266
  1142.1 243.0 %reduce-scatter.27.cloned.1.call-start = ((), (), s32[]{:S(2)}) async-start(), calls=%async_computation.23 | async-start | bytes 655360
  1143.3 274.5 %all-reduce.13.cloned.1.call-start = ((), (), s32[]{:S(2)}) async-start(), calls=%async_computation.25 | async-start | bytes 8388608 | tf_op jit(solution)/shard_map/psum | solution.py:273
  1357.2 5.7 copy-start.3
  1357.2 6.7 copy-start.8
  1417.8 6.4 copy-start.21
  1417.8 7.4 copy-start.20
  (18 other events, 16.2 us)
Sparse Core Ops, SparseCore 0:
  9.8 37.8 all-gather.7
  50.1 30.8 all-gather.9
  86.5 9.0 all-gather.11
  97.5 10.1 all-gather.17
  150.6 155.0 all-reduce.6
  307.6 34.3 all-gather.13
  343.9 35.1 all-gather.15
  391.1 154.9 all-reduce.8
  611.7 8.5 reduce-scatter.12
  623.1 10.8 reduce-scatter.14
  640.7 292.6 all-reduce.10
  1115.7 51.7 reduce-scatter.24
  1171.2 27.6 reduce-scatter.18
  1201.8 52.6 reduce-scatter.22
  1257.6 52.6 reduce-scatter.20
  1313.1 43.9 reduce-scatter.16
  1360.4 24.7 reduce-scatter.26
  1388.8 28.9 all-reduce.12
where the time goes:
time: 1440 us; the launch traced here: 1430 us
  waiting for transfers between devices  922 us (64%)
  local copies, waits for them, and re-layouts  273 us (19%)
  matrix products  141 us (10%)
  other arithmetic  53.4 us (4%)
  blocking collectives  26.7 us (2%)
  between operations  15.8 us (1%)
    psum x1, waiting for transfers between devices, body(): output = (middle + lax.psum(mlp_part, 'tp')).astype(jnp.bfloat16)  292 us
    unnamed x116, local copies, waits for them, and re-layouts  255 us
    psum x1, waiting for transfers between devices, body(): lax.psum(jnp.einsum('stf,df->std', grad_hidden, back_up, preferred_elemen...  155 us
    psum x1, waiting for transfers between devices, body(): middle = inputs_f + lax.psum(branch_part, 'tp')  154 us
    reduce_scatter x1, waiting for transfers between devices, body(): lax.psum_scatter(grad_up, 'shard', scatter_dimension=0, tiled=True)  55.8 us
    reduce_scatter x1, waiting for transfers between devices, body(): lax.psum_scatter(grad_qkv, 'shard', scatter_dimension=1, tiled=True)  46.8 us
    unnamed x20, waiting for transfers between devices  44.9 us
    all_gather x1, waiting for transfers between devices, body(): lax.all_gather(up_weight, 'shard', axis=0, tiled=True)  31 us
  transfers between devices with their start and end apart: 18, of which 14 were waited for; matrix products, arithmetic and copies ran while one was open for 10% of the time, Pallas kernels for 0%

commit v1 on v0

--- a/solution.py
+++ b/solution.py
@@ -187,7 +187,7 @@
     branch_part = jnp.einsum(
         "ste,ed->std", attended_low, full_out, preferred_element_type=jnp.float32
     )
-    middle = inputs_f + lax.psum(branch_part, "tp")
+    middle = inputs_f + jnp.sum(lax.all_gather(branch_part, "tp"), axis=0)
     second_out, normed_two, inverse_two = scaled_norm(
         middle, gains_f[1], modulation[:, 2], modulation[:, 3]
     )

time: 1440 us -> 1580 us (1.097)
  waiting for transfers between devices: 922 us -> 1040 us
    all_gather x0 -> x1, waiting for transfers between devices: none -> 286 us  [body(): middle = inputs_f + jnp.sum(lax.all_gather(branch_part, 'tp'), axis=0)]
    psum x1 -> x0, waiting for transfers between devices: 154 us -> none  [body(): middle = inputs_f + lax.psum(branch_part, 'tp')]
where the time goes in v1:
time: 1580 us; the launch traced here: 1560 us
  waiting for transfers between devices  1040 us (66%)
  local copies, waits for them, and re-layouts  273 us (17%)
  matrix products  141 us (9%)
  other arithmetic  63.7 us (4%)
  blocking collectives  26.7 us (2%)
  between operations  15.8 us (1%)
    psum x1, waiting for transfers between devices, body(): output = (middle + lax.psum(mlp_part, 'tp')).astype(jnp.bfloat16)  292 us
    all_gather x1, waiting for transfers between devices, body(): middle = inputs_f + jnp.sum(lax.all_gather(branch_part, 'tp'), axis=0)  286 us
    unnamed x116, local copies, waits for them, and re-layouts  255 us
    psum x1, waiting for transfers between devices, body(): lax.psum(jnp.einsum('stf,df->std', grad_hidden, back_up, preferred_elemen...  155 us
    reduce_scatter x1, waiting for transfers between devices, body(): lax.psum_scatter(grad_up, 'shard', scatter_dimension=0, tiled=True)  55.6 us
    reduce_scatter x1, waiting for transfers between devices, body(): lax.psum_scatter(grad_qkv, 'shard', scatter_dimension=1, tiled=True)  47.1 us
    unnamed x20, waiting for transfers between devices  45.2 us
  transfers between devices with their start and end apart: 18, of which 14 were waited for; matrix products, arithmetic and copies ran while one was open for 10% of the time, Pallas kernels for 0%

profile of v1, /device:TPU:0, one launch (start us, length us, event | category | flops | bytes accessed | tf_op | source)
XLA Modules:
  0.0 1563.7 jit_solution(8406092710572245599)
XLA Ops:
  11.3 9.6 all_gather.36
  24.3 23.4 %all-gather.10.cloned.1.call-done = bf16[256,4,1024]{2,1,0:T(4,128)(2,1)} async-done(((bf16[256,4,256]{2,1,0:T(4,128)(2,1)}), bf16[256,4,1024]{2,1,0:T(4,128)(2,1)}) %all-gather.10.cloned.1.call-update) | async-done | bytes 2097168 | tf_op jit(solution)/shard_map/all_gather | solution.py:150
  47.7 3.4 fusion.90
  51.8 29.2 %all-gather.12.cloned.1.call-done = bf16[3,1024,256]{1,2,0:T(8,128)(2,1)} async-done(((bf16[3,256,256]{1,2,0:T(8,128)(2,1)}), bf16[3,1024,256]{1,2,0:T(8,128)(2,1)}) %all-gather.12.cloned.1.call-update) | async-done | bytes 1572880 | tf_op jit(solution)/shard_map/all_gather | solution.py:146
  81.0 3.4 convolution_bitcast_fusion.4
  88.6 14.1 all_gather.41
  105.9 2.9 copy.45
  108.8 2.7 copy.43
  111.5 35.0 %while.28 = (s32[]{:T(128)}, bf16[4,1,1024,64]{2,3,1,0:T(8,128)(2,1)}, f32[4,1,1024]{2,1,0:T(1,128)S(1)}, bf16[4,1,1024,64]{3,2,1,0:T(8,128)(2,1)S(1)}, bf16[4,1...) while((s32[]{:T(128)}, bf16[4,1,1024,64]{2,3,1,0:T(8,128)(2,1)}, ...), condition=%wide.region_5.6_spmd.clone, body=%wide.region_2.5_spmd.sunk.clone | while | flops 555744256 | bytes 30976136 | solution.py:182
  111.5 2.4 multiply_reduce_fusion.14
  115.8 3.6 fusion.163
  120.2 2.4 multiply_reduce_fusion.14
  124.6 3.6 fusion.163
  129.0 2.4 multiply_reduce_fusion.14
  133.3 3.6 fusion.163
  137.7 2.4 multiply_reduce_fusion.14
  142.1 3.6 fusion.163
  146.5 3.9 fusion.114
  151.8 285.7 %all-gather.22.cloned.1.call-done = f32[4096,1024]{1,0:T(8,128)} async-done(((f32[1024,1024]{1,0:T(8,128)}), f32[4096,1024]{1,0:T(8,128)}) %all-gather.22.cloned.1.call-update) | async-done | bytes 16777232 | tf_op jit(solution)/shard_map/all_gather | solution.py:190
  437.5 10.3 reduce.19
  447.8 2.7 fusion.110
  453.1 19.7 %all-gather.16.cloned.1.call-done = bf16[1024,1024]{1,0:T(8,128)(2,1)} async-done(((bf16[256,1024]{1,0:T(8,128)(2,1)}), bf16[1024,1024]{1,0:T(8,128)(2,1)}) %all-gather.16.cloned.1.call-update) | async-done | bytes 2097168 | tf_op jit(solution)/shard_map/all_gather | solution.py:148
  472.7 15.0 fusion.66
  487.7 22.1 %all-gather.18.cloned.1.call-done = bf16[1024,1024]{1,0:T(8,128)(2,1)} async-done(((bf16[1024,256]{1,0:T(8,128)(2,1)}), bf16[1024,1024]{1,0:T(8,128)(2,1)}) %all-gather.18.cloned.1.call-update) | async-done | bytes 2097168 | tf_op jit(solution)/shard_map/all_gather | solution.py:149
  509.8 6.0 fusion.72
  517.2 4.4 convolution_bitcast_fusion.1
  521.9 154.9 %all-reduce.6.cloned.1.call-done = f32[1,1024,1024]{2,1,0:T(8,128)} async-done(((f32[1,1024,1024]{2,1,0:T(8,128)}), f32[1,1024,1024]{2,1,0:T(8,128)}) %all-reduce.6.cloned.1.call-update) | async-done | bytes 4194320 | tf_op jit(solution)/shard_map/psum | solution.py:213
  676.8 6.2 multiply_reduce_fusion.2
  688.3 2.4 copy.46
  690.6 51.6 %while.29 = (s32[]{:T(128)}, f32[4,1,1024,64]{2,3,1,0:T(8,128)}, f32[4,1,2048,64]{2,3,1,0:T(8,128)}, f32[4,1,2048,64]{2,3,1,0:T(8,128)}, bf16[4,1,1024,64]{3,2,1...) while((s32[]{:T(128)}, f32[4,1,1024,64]{2,3,1,0:T(8,128)}, ...), condition=%wide.region_15.16_spmd.clone, body=%wide.region_13.15_spmd.sunk.clone | while | flops 1367538688 | bytes 68977792 | solution.py:227
  691.9 2.5 fusion.175
  694.4 3.2 multiply_reduce_fusion.15
  704.8 2.4 fusion.175
  707.3 3.2 multiply_reduce_fusion.15
  717.7 2.4 fusion.175
  720.1 3.2 multiply_reduce_fusion.15
  730.6 2.4 fusion.175
  733.0 3.2 multiply_reduce_fusion.15
  742.3 2.9 copy.49
  745.7 7.3 convolution_bitcast_fusion.2
  755.1 9.4 reduce-scatter.15.cloned.1.call-done
  765.8 5.2 convolution_bitcast_fusion
  771.7 292.3 %all-reduce.8.cloned.1.call-done = (f32[1,1024,1024]{2,1,0:T(8,128)}, f32[1,1024,1024]{2,1,0:T(8,128)}) async-done(((f32[1,1024,1024]{2,1,0:T(8,128)}, f32[1,1024,1024]{2,1,0:T(8,128)}), (f32[1,1024,1024]{2,1,0:T(8,128)}, f32[1,1024,1024]{2,1,0:T(8,128)})) %all-reduce.8.cloned.1.call-update) | async-done | bytes 8388624 | tf_op jit(solution)/shard_map/psum | solution.py:198
  1064.0 4.2 multiply_reduce_fusion.3
  1068.3 2.6 broadcast_multiply_fusion
  1070.8 64.8 %copy.59 = f32[256,4,1024]{1,0,2:T(8,128)} copy(f32[256,4,1024]{2,1,0:T(4,128)} %broadcast_multiply_fusion) | data formatting | bytes 8388608
  1135.6 110.5 %reshape.623 = f32[1024,1024]{1,0:T(8,128)} reshape(f32[1024,256,4]{2,1,0:T(8,128)} %bitcast.87) | data formatting | bytes 8388608
  1247.2 3.9 fusion.83
  1251.1 7.2 fusion.87
  1259.1 7.7 fusion.106
  1267.9 4.8 convolution_bitcast_fusion.3
  1273.9 24.2 %reduce-scatter.25.cloned.1.call-done = f32[256,1024]{1,0:T(8,128)} async-done(((f32[1024,1024]{1,0:T(8,128)}), f32[256,1024]{1,0:T(8,128)}) %reduce-scatter.25.cloned.1.call-update) | async-done | bytes 1048592
  1298.0 36.8 %reshape.624 = f32[256,256,4]{2,1,0:T(8,128)} reshape(f32[256,1024]{1,0:T(8,128)} %reduce-scatter.25.cloned.1.call-done) | data formatting | bytes 2097152
  1334.8 21.0 %copy.60 = f32[256,4,256]{2,1,0:T(4,128)} copy(f32[256,4,256]{1,0,2:T(8,128)} %bitcast.254) | data formatting | bytes 2097152
  1355.8 29.2 %reduce-scatter.23.cloned.1.call-done = f32[1024,256]{1,0:T(8,128)} async-done(((f32[1024,1024]{1,0:T(8,128)}), f32[1024,256]{1,0:T(8,128)}) %reduce-scatter.23.cloned.1.call-update) | async-done | bytes 1048592 | tf_op jit(solution)/shard_map/reduce_scatter | solution.py:269
  1385.0 55.6 %reduce-scatter.21.cloned.1.call-done = f32[256,1024]{1,0:T(8,128)} async-done(((f32[1024,1024]{1,0:T(8,128)}), f32[256,1024]{1,0:T(8,128)}) %reduce-scatter.21.cloned.1.call-update) | async-done | bytes 1048592 | tf_op jit(solution)/shard_map/reduce_scatter | solution.py:268
  1440.6 47.1 %reduce-scatter.17.cloned.1.call-done = f32[3,256,256]{1,2,0:T(8,128)} async-done(((f32[3,1024,256]{1,2,0:T(8,128)}), f32[3,256,256]{1,2,0:T(8,128)}) %reduce-scatter.17.cloned.1.call-update) | async-done | bytes 786448 | tf_op jit(solution)/shard_map/reduce_scatter | solution.py:266
  1487.7 5.7 add_convert_fusion
  1494.4 2.5 fusion.62
  1496.9 19.0 %reduce-scatter.27.cloned.1.call-done = f32[256,2]{1,0:T(8,128)} async-done(((f32[1024,2]{1,0:T(8,128)}), f32[256,2]{1,0:T(8,128)}) %reduce-scatter.27.cloned.1.call-update) | async-done | bytes 2064
  1516.9 3.0 psum.71
  1520.0 28.3 %all-reduce.10.cloned.1.call-done = (f32[3,256,256]{1,2,0:T(8,128)}, f32[256,256]{1,0:T(8,128)}, f32[256,1024]{1,0:T(8,128)}, f32[1024,256]{1,0:T(8,128)}, f32[256,4,256]{2,1,0:T(4,128)}) async-done(((f32[3,256,256]{1,2,0:T(8,128)}, f32[256,256]{1,0:T(8,128)}, f32[256,1024]{1,0:T(8,128)}, f32[1024,256]{1,0:T(8,128)}, f32[256,4,256]{2,1,0:T(4,128)}), (f32[3,256,256]{1,2,0:T(8,128)}, f32[256,256]{1,0:T(8,128)}, ...) | async-done | bytes 4194320 | tf_op jit(solution)/shard_map/psum | solution.py:273
  1548.3 2.4 copy.54
  1552.4 2.3 copy.107
  (247 shorter events, 79.5 us)
Async XLA Ops:
  7.2 15.8 %copy-start.4 = (bf16[1,1024,1024]{2,1,0:T(8,128)(2,1)S(1)}, bf16[1,1024,1024]{2,1,0:T(8,128)(2,1)}, u32[]{:S(2)}) copy-start(bf16[1,1024,1024]{2,1,0:T(8,128)(2,1)} %param.14) | copy-start | bytes 6291460
  7.2 40.6 %all-gather.10.cloned.1.call-start = ((), (), s32[]{:S(2)}) async-start(), calls=%async_computation.8 | async-start | bytes 2621440 | tf_op jit(solution)/shard_map/all_gather | solution.py:150
  7.9 73.1 %all-gather.12.cloned.1.call-start = ((), (), s32[]{:S(2)}) async-start(), calls=%async_computation.9 | async-start | bytes 1966080 | tf_op jit(solution)/shard_map/all_gather | solution.py:146
  9.9 96.0 %all-gather.14.cloned.1.call-start = ((), (), s32[]{:S(2)}) async-start(), calls=%async_computation.10 | async-start | bytes 1572864 | tf_op jit(solution)/shard_map/all_gather | solution.py:178
  21.0 26.8 %copy-start.51 = (f32[1,128]{1,0:T(1,128)}, f32[1,128]{1,0:T(1,128)S(1)}, u32[]{:S(2)}) copy-start(f32[1,128]{1,0:T(1,128)S(1)} %get-tuple-element.244) | copy-start | bytes 1540
  21.0 30.2 %copy-start.49 = (f32[1,128]{1,0:T(1,128)}, f32[1,128]{1,0:T(1,128)S(1)}, u32[]{:S(2)}) copy-start(f32[1,128]{1,0:T(1,128)S(1)} %get-tuple-element.243) | copy-start | bytes 1540
  23.0 61.4 %copy-start.29 = (f32[1024]{0:T(1024)}, f32[1024]{0:T(1024)S(1)}, u32[]{:S(2)}) copy-start(f32[1024]{0:T(1024)S(1)} %broadcast_multiply_fusion.6) | copy-start | bytes 12292
  23.7 60.7 %copy-start.33 = (f32[1024]{0:T(1024)}, f32[1024]{0:T(1024)S(1)}, u32[]{:S(2)}) copy-start(f32[1024]{0:T(1024)S(1)} %add_rsqrt_fusion.1) | copy-start | bytes 12292
  23.8 60.7 %copy-start.41 = (f32[1,1024]{1,0:T(1,128)}, f32[1,1024]{1,0:T(1,128)S(1)}, u32[]{:S(2)}) copy-start(f32[1,1024]{1,0:T(1,128)S(1)} %get-tuple-element.240) | copy-start | bytes 12292
  23.8 653.0 %copy-start.36 = (f32[1,1024]{1,0:T(1,128)}, f32[1,1024]{1,0:T(1,128)S(1)}, u32[]{:S(2)}) copy-start(f32[1,1024]{1,0:T(1,128)S(1)} %get-tuple-element.239) | copy-start | bytes 12292
  24.3 60.4 %copy-start.16 = (f32[1024,32]{0,1:T(8,128)}, f32[1024,32]{0,1:T(8,128)S(1)}, u32[]{:S(2)}) copy-start(f32[1024,32]{0,1:T(8,128)S(1)} %get-tuple-element.237) | copy-start | bytes 393220
  24.3 60.4 %copy-start.18 = (f32[1024,32]{0,1:T(8,128)}, f32[1024,32]{0,1:T(8,128)S(1)}, u32[]{:S(2)}) copy-start(f32[1024,32]{0,1:T(8,128)S(1)} %get-tuple-element.238) | copy-start | bytes 393220
  51.2 33.3 %copy-start.45 = (f32[1,1,1024]{2,0,1:T(1,128)}, f32[1,1,1024]{2,0,1:T(1,128)S(1)}, u32[]{:S(2)}) copy-start(f32[1,1,1024]{2,0,1:T(1,128)S(1)} %get-tuple-element.236) | copy-start | bytes 12292
  51.2 421.5 %copy-start.47 = (f32[1,1,1024]{2,0,1:T(1,128)}, f32[1,1,1024]{2,0,1:T(1,128)S(1)}, u32[]{:S(2)}) copy-start(f32[1,1,1024]{2,0,1:T(1,128)S(1)} %get-tuple-element.235) | copy-start | bytes 12292
  51.8 32.6 %copy-start.43 = (f32[1,1,1024]{2,1,0:T(1,128)}, f32[1,1,1024]{2,1,0:T(1,128)S(1)}, u32[]{:S(2)}) copy-start(f32[1,1,1024]{2,1,0:T(1,128)S(1)} %get-tuple-element.234) | copy-start | bytes 12292
  51.8 624.9 %copy-start.39 = (f32[1,1,1024]{2,1,0:T(1,128)}, f32[1,1,1024]{2,1,0:T(1,128)S(1)}, u32[]{:S(2)}) copy-start(f32[1,1,1024]{2,1,0:T(1,128)S(1)} %get-tuple-element.233) | copy-start | bytes 12292
  84.5 1.8 copy-start.14
  84.7 3.8 copy-start.26
  86.3 22.4 %all-gather.20.cloned.1.call-start = ((), (), s32[]{:S(2)}) async-start(), calls=%async_computation.20 | async-start | bytes 1572864 | tf_op jit(solution)/shard_map/all_gather | solution.py:179
  88.5 349.0 %all-gather.22.cloned.1.call-start = ((), (), s32[]{:S(2)}) async-start(), calls=%async_computation.21 | async-start | bytes 20971520 | tf_op jit(solution)/shard_map/all_gather | solution.py:190
  113.9 2.0 copy-start.10
  122.6 2.0 copy-start.10
  131.4 2.0 copy-start.10
  140.1 2.0 copy-start.10
  150.4 322.3 %all-gather.16.cloned.1.call-start = ((), (), s32[]{:S(2)}) async-start(), calls=%async_computation.11 | async-start | bytes 2621440 | tf_op jit(solution)/shard_map/all_gather | solution.py:148
  151.0 358.7 %all-gather.18.cloned.1.call-start = ((), (), s32[]{:S(2)}) async-start(), calls=%async_computation.12 | async-start | bytes 2621440 | tf_op jit(solution)/shard_map/all_gather | solution.py:149
  151.8 525.0 %all-reduce.6.cloned.1.call-start = ((), (), s32[]{:S(2)}) async-start(), calls=%async_computation.13 | async-start | bytes 8388608 | tf_op jit(solution)/shard_map/psum | solution.py:213
  450.5 2.0 copy-start
  450.5 232.5 %copy-start.27 = (f32[1024]{0:T(1024)}, f32[1024]{0:T(1024)S(1)}, u32[]{:S(2)}) copy-start(f32[1024]{0:T(1024)S(1)} %broadcast_multiply_fusion.5) | copy-start | bytes 12292
  453.1 230.0 %copy-start.31 = (f32[1024]{0:T(1024)}, f32[1024]{0:T(1024)S(1)}, u32[]{:S(2)}) copy-start(f32[1024]{0:T(1024)S(1)} %add_rsqrt_fusion) | copy-start | bytes 12292
  472.7 37.0 %copy-start.15 = (bf16[1,1024,1024]{2,1,0:T(8,128)(2,1)S(1)}, bf16[1,1024,1024]{2,1,0:T(8,128)(2,1)}, u32[]{:S(2)}) copy-start(bf16[1,1024,1024]{2,1,0:T(8,128)(2,1)} %param.23) | copy-start | bytes 6291460
  509.8 7.4 copy-start.53
  515.8 1.4 copy-start.54
  521.6 231.4 %reduce-scatter.13.cloned.1.call-start = ((), (), s32[]{:S(2)}) async-start(), calls=%async_computation.14 | async-start | bytes 3145728 | tf_op jit(solution)/shard_map/reduce_scatter | solution.py:240
  676.8 6.3 copy-start.1
  676.8 6.3 copy-start.7
  683.0 3.7 copy-start.13
  684.7 2.0 copy-start.2
  686.7 3.9 copy-start.6
  742.3 22.2 %reduce-scatter.15.cloned.1.call-start = ((), (), s32[]{:S(2)}) async-start(), calls=%async_computation.15 | async-start | bytes 3145728 | tf_op jit(solution)/shard_map/reduce_scatter | solution.py:241
  745.2 318.8 %all-reduce.8.cloned.1.call-start = ((), (), s32[]{:S(2)}) async-start(), calls=%async_computation.24 | async-start | bytes 16777216 | tf_op jit(solution)/shard_map/psum | solution.py:198
  745.7 7.3 copy-start.17
  745.7 7.3 copy-start.19
  745.7 7.3 copy-start.22
  754.8 16.2 %copy-start.23 = (bf16[1,1024,256]{2,1,0:T(8,128)(2,1)}, bf16[1,1024,256]{2,1,0:T(8,128)(2,1)S(1)}, u32[]{:S(2)}) copy-start(bf16[1,1024,256]{2,1,0:T(8,128)(2,1)S(1)} %copy.50) | copy-start | bytes 1572868
  755.1 16.0 %copy-start.25 = (bf16[1,1024,256]{2,1,0:T(8,128)(2,1)}, bf16[1,1024,256]{2,1,0:T(8,128)(2,1)S(1)}, u32[]{:S(2)}) copy-start(bf16[1,1024,256]{2,1,0:T(8,128)(2,1)S(1)} %copy.51) | copy-start | bytes 1572868
  771.0 293.0 %copy-start.5 = (bf16[1,1024,1024]{2,1,0:T(8,128)(2,1)S(1)}, bf16[1,1024,1024]{2,1,0:T(8,128)(2,1)}, u32[]{:S(2)}) copy-start(bf16[1,1024,1024]{2,1,0:T(8,128)(2,1)} %param.14) | copy-start | bytes 6291460
  771.1 293.0 %copy-start.30 = (f32[1024]{0:T(1024)S(1)}, f32[1024]{0:T(1024)}, u32[]{:S(2)}) copy-start(f32[1024]{0:T(1024)} %copy-done.29) | copy-start | bytes 12292
  771.1 292.9 %copy-start.34 = (f32[1024]{0:T(1024)S(1)}, f32[1024]{0:T(1024)}, u32[]{:S(2)}) copy-start(f32[1024]{0:T(1024)} %copy-done.33) | copy-start | bytes 12292
  771.1 292.9 %copy-start.35 = (f32[1,1,1024]{2,1,0:T(1,128)S(1)}, f32[1,1,1024]{2,1,0:T(1,128)}, u32[]{:S(2)}) copy-start(f32[1,1,1024]{2,1,0:T(1,128)} %get-tuple-element.231) | copy-start | bytes 12292
  771.1 292.9 %copy-start.42 = (f32[1,1024]{1,0:T(1,128)S(1)}, f32[1,1024]{1,0:T(1,128)}, u32[]{:S(2)}) copy-start(f32[1,1024]{1,0:T(1,128)} %copy-done.41) | copy-start | bytes 12292
  771.1 292.9 %copy-start.44 = (f32[1,1,1024]{2,1,0:T(1,128)S(1)}, f32[1,1,1024]{2,1,0:T(1,128)}, u32[]{:S(2)}) copy-start(f32[1,1,1024]{2,1,0:T(1,128)} %copy-done.43) | copy-start | bytes 12292
  771.1 526.9 %reduce-scatter.25.cloned.1.call-start = ((), (), s32[]{:S(2)}) async-start(), calls=%async_computation.22 | async-start | bytes 5242880
  1246.2 109.7 %reduce-scatter.19.cloned.1.call-start = ((), (), s32[]{:S(2)}) async-start(), calls=%async_computation.17 | async-start | bytes 1310720 | tf_op jit(solution)/shard_map/reduce_scatter | solution.py:267
  1251.1 134.0 %reduce-scatter.23.cloned.1.call-start = ((), (), s32[]{:S(2)}) async-start(), calls=%async_computation.19 | async-start | bytes 5242880 | tf_op jit(solution)/shard_map/reduce_scatter | solution.py:269
  1258.4 182.2 %reduce-scatter.21.cloned.1.call-start = ((), (), s32[]{:S(2)}) async-start(), calls=%async_computation.18 | async-start | bytes 5242880 | tf_op jit(solution)/shard_map/reduce_scatter | solution.py:268
  1266.8 5.9 copy-start.38
  1266.8 220.8 %reduce-scatter.17.cloned.1.call-start = ((), (), s32[]{:S(2)}) async-start(), calls=%async_computation.16 | async-start | bytes 3932160 | tf_op jit(solution)/shard_map/reduce_scatter | solution.py:266
  1272.7 243.3 %reduce-scatter.27.cloned.1.call-start = ((), (), s32[]{:S(2)}) async-start(), calls=%async_computation.23 | async-start | bytes 655360
  1273.8 274.5 %all-reduce.10.cloned.1.call-start = ((), (), s32[]{:S(2)}) async-start(), calls=%async_computation.25 | async-start | bytes 8388608 | tf_op jit(solution)/shard_map/psum | solution.py:273
  1487.7 5.7 copy-start.3
  1487.7 6.7 copy-start.8
  1548.3 6.4 copy-start.21
  1548.3 7.4 copy-start.20
  (18 other events, 16.2 us)
Sparse Core Ops, SparseCore 0:
  9.8 37.8 all-gather.9
  50.1 30.8 all-gather.11
  86.5 9.0 all-gather.13
  97.5 10.1 all-gather.19
  150.6 286.9 all-gather.21
  439.2 33.4 all-gather.15
  474.6 35.1 all-gather.17
  521.7 154.9 all-reduce.5
  742.4 8.5 reduce-scatter.12
  753.7 10.7 reduce-scatter.14
  771.3 292.7 all-reduce.7
  1246.3 51.7 reduce-scatter.24
  1301.5 27.7 reduce-scatter.18
  1332.4 52.6 reduce-scatter.22
  1387.9 52.6 reduce-scatter.20
  1443.7 43.9 reduce-scatter.16
  1491.1 24.7 reduce-scatter.26
  1519.4 28.8 all-reduce.9
